TPU v7x, 512 devices: a whole 4x8x8 slice. The times are simulated.
512 devices in a mesh: edp: 16 (over z, core), ep: 32 (over y, x).
Axes of the slice: x: 4, y: 8, z: 8, core: 2. Of those that a mesh axis runs over, the one named last changes fastest.
Arguments:
- token_acts: bfloat16 [16, 32, 2, 64, 1024], P('edp', 'ep'), may hold values from -6 to 6
- out_grad: bfloat16 [16, 32, 3584, 128], P('edp', 'ep'), may hold values from -0.59765625 to 0.59765625
- counts: int32 [16, 32, 2], P('edp', 'ep'), may hold values from 1 to 64, as said below
- params: float32 [32, 3584, 1024], P('ep', 'edp'), may hold values from -3 to 3
- first_moment: bfloat16 [32, 3584, 1024], P('ep', 'edp'), may hold values from -3 to 3
- second_moment: bfloat16 [32, 3584, 1024], P('ep', 'edp'), may hold values from 0.049804688 to 2
- old_expert: int32 [32], replicated, may hold values from 0 to 31, each once
- replica_of: int32 [32], replicated, may hold values from 0 to 31
- new_expert: int32 [32], replicated, may hold values from 0 to 31, each once
Outputs:
- update_step: float32 [32, 3584, 1024], P('ep', 'edp')
- new_first: bfloat16 [32, 3584, 1024], P('ep', 'edp')
- new_second: bfloat16 [32, 3584, 1024], P('ep', 'edp')
Inputs may be any that keep to these rules, and one draw needn't show every extreme that they name: `counts`: every slot has at least one live token; some slot is full and some slot has exactly one live token in every draw. `old_expert`: each expert appears exactly once. `new_expert`: each expert appears exactly once. `replica_of`: any expert may be served by any number of replica slots, its owner's included.
All inputs are finite; a program needn't handle non-finite values.
Results may differ from a plain program's by a relative error of at most 0.015.
Values may be sent and summed in bfloat16 or wider, within the bound.
A program may use at most 64 MiB of HBM per device.

v0:
```python
import jax
import jax.numpy as jnp
from jax import lax
from jax.sharding import PartitionSpec as P

beta_one = 0.9
beta_two = 0.95
bias_one = 0.9999734386011124
bias_two = 0.994079470779666
decay_rate = 0.1
adam_eps = 1e-08


def adam_update(weights, first_old, second_old, gradient):
    first_new = beta_one * first_old.astype(jnp.float32) + (1.0 - beta_one) * gradient
    second_new = beta_two * second_old.astype(jnp.float32) + (1.0 - beta_two) * gradient * gradient
    scaled = first_new / bias_one / (jnp.sqrt(second_new / bias_two) + adam_eps)
    step_new = -(scaled + decay_rate * weights)
    return (step_new, first_new.astype(jnp.bfloat16), second_new.astype(jnp.bfloat16))


def local(
    token_acts,
    out_grad,
    counts,
    params,
    first_moment,
    second_moment,
    old_expert,
    replica_of,
    new_expert,
):
    groups = lax.axis_size("edp")
    owners = lax.axis_size("ep")
    model_width = out_grad.shape[2]
    slot_count = token_acts.shape[2]
    tok_slot = token_acts.shape[3]
    hidden_units = token_acts.shape[4]
    row_count = model_width // groups
    piece_len = row_count * hidden_units // owners
    local_grad = out_grad[0, 0]
    local_counts = counts[0, 0]
    column = jnp.arange(slot_count * tok_slot, dtype=jnp.int32)
    slot_index = column // tok_slot
    live_limit = jnp.where(slot_index == 0, local_counts[0], local_counts[1])
    live_mask = column % tok_slot < live_limit
    masked = jnp.where(live_mask[None, :], local_grad, jnp.zeros_like(local_grad))
    received = lax.all_to_all(
        masked.reshape(groups, row_count, slot_count * tok_slot),
        "edp",
        split_axis=0,
        concat_axis=0,
        tiled=True,
    )
    arrived = lax.all_gather(token_acts[0], "edp", axis=0, tiled=True)
    count_here = arrived.shape[0]
    grad_block = received
    grad_block = grad_block.reshape(count_here, row_count, slot_count, tok_slot)
    slot_grads = jnp.einsum(
        "adst,astf->sdf", grad_block, arrived, preferred_element_type=jnp.float32
    )
    own_grad = slot_grads[0].reshape(owners, piece_len)
    replica_grad = slot_grads[1].reshape(owners, piece_len)
    sum_matrix = (replica_of[None, :] == old_expert[:, None]).astype(jnp.float32)
    move_matrix = (old_expert[None, :] == new_expert[:, None]).astype(jnp.float32)
    weights = params[0].reshape(owners, piece_len)
    first_old = first_moment[0].reshape(owners, piece_len)
    second_old = second_moment[0].reshape(owners, piece_len)
    replica_sent = lax.all_to_all(
        replica_grad.astype(jnp.bfloat16), "ep", split_axis=0, concat_axis=0, tiled=True
    ).astype(replica_grad.dtype)
    set_sums = jnp.dot(sum_matrix, replica_sent, precision=lax.Precision.HIGHEST)
    returned = lax.all_to_all(
        set_sums.astype(jnp.bfloat16), "ep", split_axis=0, concat_axis=0, tiled=True
    ).astype(set_sums.dtype)
    weights, first_old, second_old = adam_update(
        weights, first_old, second_old, own_grad + returned
    )
    weight_pieces = lax.all_to_all(weights, "ep", split_axis=0, concat_axis=0, tiled=True)
    first_pieces, second_pieces = (
        lax.all_to_all(first_old, "ep", split_axis=0, concat_axis=0, tiled=True),
        lax.all_to_all(second_old, "ep", split_axis=0, concat_axis=0, tiled=True),
    )
    placed_steps = jnp.dot(move_matrix, weight_pieces, precision=lax.Precision.HIGHEST)
    move_half = move_matrix.astype(jnp.bfloat16)
    placed_first = jnp.dot(move_half, first_pieces, preferred_element_type=jnp.float32).astype(
        jnp.bfloat16
    )
    placed_second = jnp.dot(move_half, second_pieces, preferred_element_type=jnp.float32).astype(
        jnp.bfloat16
    )
    final_steps = lax.all_to_all(placed_steps, "ep", split_axis=0, concat_axis=0, tiled=True)
    final_first, final_second = (
        lax.all_to_all(placed_first, "ep", split_axis=0, concat_axis=0, tiled=True),
        lax.all_to_all(placed_second, "ep", split_axis=0, concat_axis=0, tiled=True),
    )
    return (
        final_steps.reshape(1, row_count, hidden_units),
        final_first.reshape(1, row_count, hidden_units),
        final_second.reshape(1, row_count, hidden_units),
    )


def solution(mesh):
    return jax.shard_map(
        local,
        mesh=mesh,
        in_specs=(
            P("edp", "ep", None, None, None),
            P("edp", "ep", None, None),
            P("edp", "ep", None),
            P("ep", "edp", None),
            P("ep", "edp", None),
            P("ep", "edp", None),
            P(),
            P(),
            P(),
        ),
        out_specs=(P("ep", "edp", None), P("ep", "edp", None), P("ep", "edp", None)),
        check_vma=False,
    )
```

profile of v0, /device:TPU:2, one launch (start us, length us, event | category | flops | bytes accessed | tf_op | source)
XLA Modules:
  0.0 280.3 jit_solution(12393630941862970195)
XLA Ops:
  11.8 41.0 %all_to_all.77 = bf16[16,224,128]{2,1,0:T(8,128)(2,1)S(1)} all-to-all(bf16[16,224,128]{2,1,0:T(8,128)(2,1)S(1)} %broadcast_select_fusion), channel_id=1, replica_groups=mesh['edp'=16,'ep'=32] {'edp'}, dimensions={0} | all-to-all | bytes 1835008 | tf_op jit(solution)/shard_map/all_to_all | solution.py:48
  53.3 18.0 %all-gather.3.cloned.1.call-done = bf16[16,1,2,64,1024]{4,3,2,1,0:T(8,128)(2,1)} async-done(((bf16[1,1,2,64,1024]{4,3,2,1,0:T(8,128)(2,1)}), bf16[16,1,2,64,1024]{4,3,2,1,0:T(8,128)(2,1)}) %all-gather.3.cloned.1.call-update) | async-done | bytes 4194320 | tf_op jit(solution)/shard_map/all_gather | solution.py:55
  71.3 3.3 %fusion.5 = f32[2,224,1024]{2,1,0:T(8,128)S(1)} fusion(bf16[16,224,2,64]{1,3,2,0:T(8,128)(2,1)S(1)} %bitcast.32, bf16[16,1,2,64,1024]{4,3,2,1,0:T(8,128)(2,1)} %all-gather.3.cloned.1.call-done), kind=kOutput, calls=%fused_computation.9 | convolution fusion | flops 939524096 | bytes 6946816 | tf_op jit(solution)/shard_map/adst,astf->sdf/dot_general | solution.py:59
  75.7 3.3 %reduce.3 = bf16[32,7168]{1,0:T(8,128)(2,1)S(1)} reduce(bf16[32,1,7168]{2,1,0:T(2,128)(2,1)S(1)} %convert_element_type.77, bf16[]{:T(256)} %broadcast.125), dimensions={1}, to_apply=%convert_element_type.77.reduce_sub_computation | reduce | bytes 917506 | tf_op jit(solution)/shard_map/convert_element_type | solution.py:70
  79.3 25.9 %all_to_all.78 = bf16[32,2,3584]{2,1,0:T(2,128)(2,1)S(1)} all-to-all(bf16[32,2,3584]{2,1,0:T(2,128)(2,1)S(1)} %reshape.144), channel_id=1, replica_groups=mesh['edp'=16,'ep'=32] {'ep'}, dimensions={0} | all-to-all | bytes 917504 | tf_op jit(solution)/shard_map/all_to_all | solution.py:69
  107.8 5.6 %all-to-all-start.2 = ((bf16[32,2,3584]{2,1,0:T(2,128)(2,1)}), bf16[32,2,3584]{2,1,0:T(2,128)(2,1)S(1)}, u32[]{:S(2)}, u32[]{:S(2)}) async-start(bf16[32,2,3584]{2,1,0:T(2,128)(2,1)} %reshape.146), calls=%async_computation.2 | async-start | bytes 917504 | tf_op jit(solution)/shard_map/all_to_all | solution.py:73
  113.4 2.2 broadcast_multiply_fusion
  115.7 1.6 mul.76
  117.2 2.1 convert_multiply_fusion.1
  119.3 2.6 mul.67
  121.9 2.0 convert_multiply_fusion
  123.9 2.5 mul.71
  127.4 1.6 reshape_squeeze.2
  130.2 3.1 %fusion.32 = (bf16[32,1,7168]{2,0,1:T(8,128)(2,1)}, f32[32,1,7168]{2,0,1:T(8,128)S(1)}, bf16[32,1,7168]{2,0,1:T(8,128)(2,1)S(1)}) fusion(f32[32,1,7168]{2,0,1:T(8,128)} %mul.71, f32[32,1,7168]{2,0,1:T(8,128)S(1)} %reshape_squeeze.2, bf16[32,1,7168]{2,1,0:T(2,128)(2,1)} %reshape.147, f32[32,1,7168]{2,0,1:T(8,128)S(1)} %mul.76, f32[32,1,7168]{2,0,1:T(8,128)} %mul.67), kind=kLoop, calls=%fused_computation.47 | loop fusion | flops 3440640 | bytes 5963776 | tf_op jit(solution)/shard_map/convert_element_type | solution.py:19
  133.3 1.9 reduce.7
  136.3 9.8 %all-to-all-start.7 = ((bf16[32,2,3584]{2,1,0:T(2,128)(2,1)}), bf16[32,2,3584]{2,1,0:T(2,128)(2,1)S(1)}, u32[]{:S(2)}, u32[]{:S(2)}) async-start(bf16[32,2,3584]{2,1,0:T(2,128)(2,1)} %reshape.152), calls=%async_computation.7 | async-start | bytes 917504 | tf_op jit(solution)/shard_map/all_to_all | solution.py:82
  148.0 12.1 %all-to-all-done.7 = bf16[32,2,3584]{2,1,0:T(2,128)(2,1)S(1)} async-done(((bf16[32,2,3584]{2,1,0:T(2,128)(2,1)}), bf16[32,2,3584]{2,1,0:T(2,128)(2,1)S(1)}, u32[]{:S(2)}, u32[]{:S(2)}) %all-to-all-start.7) | async-done | bytes 458784 | tf_op jit(solution)/shard_map/all_to_all | solution.py:82
  160.1 5.7 %all-to-all-start.5 = ((bf16[32,2,3584]{2,1,0:T(2,128)(2,1)}), bf16[32,2,3584]{2,1,0:T(2,128)(2,1)S(1)}, u32[]{:S(2)}, u32[]{:S(2)}) async-start(bf16[32,2,3584]{2,1,0:T(2,128)(2,1)} %reshape.148), calls=%async_computation.5 | async-start | bytes 917504 | tf_op jit(solution)/shard_map/all_to_all | solution.py:81
  168.6 10.7 %all-to-all-done.5 = bf16[32,2,3584]{2,1,0:T(2,128)(2,1)S(1)} async-done(((bf16[32,2,3584]{2,1,0:T(2,128)(2,1)}), bf16[32,2,3584]{2,1,0:T(2,128)(2,1)S(1)}, u32[]{:S(2)}, u32[]{:S(2)}) %all-to-all-start.5) | async-done | bytes 458784 | tf_op jit(solution)/shard_map/all_to_all | solution.py:81
  179.3 5.6 %all-to-all-start.8 = ((bf16[32,2,3584]{2,1,0:T(2,128)(2,1)}), bf16[32,2,3584]{2,1,0:T(2,128)(2,1)S(1)}, u32[]{:S(2)}, u32[]{:S(2)}) async-start(bf16[32,2,3584]{2,1,0:T(2,128)(2,1)} %reshape.154), calls=%async_computation.8 | async-start | bytes 917504 | tf_op jit(solution)/shard_map/all_to_all | solution.py:95
  184.9 1.9 copy.35
  186.7 11.1 %all-to-all-done.8 = bf16[32,2,3584]{2,1,0:T(2,128)(2,1)S(1)} async-done(((bf16[32,2,3584]{2,1,0:T(2,128)(2,1)}), bf16[32,2,3584]{2,1,0:T(2,128)(2,1)S(1)}, u32[]{:S(2)}, u32[]{:S(2)}) %all-to-all-start.8) | async-done | bytes 458784 | tf_op jit(solution)/shard_map/all_to_all | solution.py:95
  197.9 5.6 %all-to-all-start.3 = ((f32[32,1,7168]{2,1,0:T(1,128)}), f32[32,1,7168]{2,1,0:T(1,128)S(1)}, u32[]{:S(2)}, u32[]{:S(2)}) async-start(f32[32,1,7168]{2,1,0:T(1,128)} %copy.35), calls=%async_computation.3 | async-start | bytes 1835008 | tf_op jit(solution)/shard_map/all_to_all | solution.py:79
  206.1 19.8 %all-to-all-done.3 = f32[32,1,7168]{2,1,0:T(1,128)S(1)} async-done(((f32[32,1,7168]{2,1,0:T(1,128)}), f32[32,1,7168]{2,1,0:T(1,128)S(1)}, u32[]{:S(2)}, u32[]{:S(2)}) %all-to-all-start.3) | async-done | bytes 917536 | tf_op jit(solution)/shard_map/all_to_all | solution.py:79
  225.9 5.6 %all-to-all-start.6 = ((bf16[32,2,3584]{2,1,0:T(2,128)(2,1)}), bf16[32,2,3584]{2,1,0:T(2,128)(2,1)S(1)}, u32[]{:S(2)}, u32[]{:S(2)}) async-start(bf16[32,2,3584]{2,1,0:T(2,128)(2,1)} %reshape.150), calls=%async_computation.6 | async-start | bytes 917504 | tf_op jit(solution)/shard_map/all_to_all | solution.py:94
  232.1 1.9 copy.36
  234.0 9.8 %all-to-all-done.6 = bf16[32,2,3584]{2,1,0:T(2,128)(2,1)S(1)} async-done(((bf16[32,2,3584]{2,1,0:T(2,128)(2,1)}), bf16[32,2,3584]{2,1,0:T(2,128)(2,1)S(1)}, u32[]{:S(2)}, u32[]{:S(2)}) %all-to-all-start.6) | async-done | bytes 458784 | tf_op jit(solution)/shard_map/all_to_all | solution.py:94
  243.7 5.6 %all-to-all-start.4 = ((f32[32,1,7168]{2,1,0:T(1,128)}), f32[32,1,7168]{2,1,0:T(1,128)S(1)}, u32[]{:S(2)}, u32[]{:S(2)}) async-start(f32[32,1,7168]{2,1,0:T(1,128)} %copy.36), calls=%async_computation.4 | async-start | bytes 1835008 | tf_op jit(solution)/shard_map/all_to_all | solution.py:92
  249.7 2.7 reduce.2
  254.1 2.7 reduce.1
  258.1 12.1 %all-to-all-done.4 = f32[32,1,7168]{2,1,0:T(1,128)S(1)} async-done(((f32[32,1,7168]{2,1,0:T(1,128)}), f32[32,1,7168]{2,1,0:T(1,128)S(1)}, u32[]{:S(2)}, u32[]{:S(2)}) %all-to-all-start.4) | async-done | bytes 917536 | tf_op jit(solution)/shard_map/all_to_all | solution.py:92
  270.2 2.2 reduce
  (40 shorter events, 24.5 us)
Async XLA Ops:
  7.2 64.1 %all-gather.3.cloned.1.call-start = ((), (), s32[]{:S(2)}) async-start(), calls=%async_computation.9 | async-start | bytes 4456448 | tf_op jit(solution)/shard_map/all_gather | solution.py:55
  74.7 30.9 %copy-start = (s32[32]{0:T(128)S(1)}, s32[32]{0:T(128)}, u32[]{:S(2)}) copy-start(s32[32]{0:T(128)} %param.15) | copy-start | bytes 388
  74.7 30.9 %copy-start.2 = (s32[32]{0:T(128)S(1)}, s32[32]{0:T(128)}, u32[]{:S(2)}) copy-start(s32[32]{0:T(128)} %param.16) | copy-start | bytes 388
  107.8 21.2 %all-to-all-start.2 = ((bf16[32,2,3584]{2,1,0:T(2,128)(2,1)}), bf16[32,2,3584]{2,1,0:T(2,128)(2,1)S(1)}, u32[]{:S(2)}, u32[]{:S(2)}) async-start(bf16[32,2,3584]{2,1,0:T(2,128)(2,1)} %reshape.146), calls=%async_computation.2 | async-start | bytes 917504 | tf_op jit(solution)/shard_map/all_to_all | solution.py:73
  133.3 33.0 %copy-start.1 = (s32[32]{0:T(128)S(1)}, s32[32]{0:T(128)}, u32[]{:S(2)}) copy-start(s32[32]{0:T(128)} %param.17) | copy-start | bytes 388
  136.3 23.9 %all-to-all-start.7 = ((bf16[32,2,3584]{2,1,0:T(2,128)(2,1)}), bf16[32,2,3584]{2,1,0:T(2,128)(2,1)S(1)}, u32[]{:S(2)}, u32[]{:S(2)}) async-start(bf16[32,2,3584]{2,1,0:T(2,128)(2,1)} %reshape.152), calls=%async_computation.7 | async-start | bytes 917504 | tf_op jit(solution)/shard_map/all_to_all | solution.py:82
  160.1 19.2 %all-to-all-start.5 = ((bf16[32,2,3584]{2,1,0:T(2,128)(2,1)}), bf16[32,2,3584]{2,1,0:T(2,128)(2,1)S(1)}, u32[]{:S(2)}, u32[]{:S(2)}) async-start(bf16[32,2,3584]{2,1,0:T(2,128)(2,1)} %reshape.148), calls=%async_computation.5 | async-start | bytes 917504 | tf_op jit(solution)/shard_map/all_to_all | solution.py:81
  179.3 18.6 %all-to-all-start.8 = ((bf16[32,2,3584]{2,1,0:T(2,128)(2,1)}), bf16[32,2,3584]{2,1,0:T(2,128)(2,1)S(1)}, u32[]{:S(2)}, u32[]{:S(2)}) async-start(bf16[32,2,3584]{2,1,0:T(2,128)(2,1)} %reshape.154), calls=%async_computation.8 | async-start | bytes 917504 | tf_op jit(solution)/shard_map/all_to_all | solution.py:95
  197.9 28.0 %all-to-all-start.3 = ((f32[32,1,7168]{2,1,0:T(1,128)}), f32[32,1,7168]{2,1,0:T(1,128)S(1)}, u32[]{:S(2)}, u32[]{:S(2)}) async-start(f32[32,1,7168]{2,1,0:T(1,128)} %copy.35), calls=%async_computation.3 | async-start | bytes 1835008 | tf_op jit(solution)/shard_map/all_to_all | solution.py:79
  225.9 17.8 %all-to-all-start.6 = ((bf16[32,2,3584]{2,1,0:T(2,128)(2,1)}), bf16[32,2,3584]{2,1,0:T(2,128)(2,1)S(1)}, u32[]{:S(2)}, u32[]{:S(2)}) async-start(bf16[32,2,3584]{2,1,0:T(2,128)(2,1)} %reshape.150), calls=%async_computation.6 | async-start | bytes 917504 | tf_op jit(solution)/shard_map/all_to_all | solution.py:94
  243.7 26.5 %all-to-all-start.4 = ((f32[32,1,7168]{2,1,0:T(1,128)}), f32[32,1,7168]{2,1,0:T(1,128)S(1)}, u32[]{:S(2)}, u32[]{:S(2)}) async-start(f32[32,1,7168]{2,1,0:T(1,128)} %copy.36), calls=%async_computation.4 | async-start | bytes 1835008 | tf_op jit(solution)/shard_map/all_to_all | solution.py:92
Sparse Core Ops, SparseCore 0:
  10.1 61.1 all-gather.2
where the time goes:
time: 282 us; the launch traced here: 280 us
  waiting for transfers between devices  94.3 us (33%)
  blocking collectives  66.9 us (24%)
  starting transfers between devices  43.4 us (15%)
  local copies, waits for them, and re-layouts  28.2 us (10%)
  other arithmetic  28.2 us (10%)
  between operations  14.3 us (5%)
  matrix products  4.97 us (2%)
    all_to_all x1, blocking collectives, local(): lax.all_to_all(masked.reshape(groups, row_count, slot_count * tok_slot),...  41 us
    all_to_all x1, blocking collectives, local(): lax.all_to_all(replica_grad.astype(jnp.bfloat16), 'ep', split_axis=0, con...  25.9 us
    all_to_all x1, waiting for transfers between devices, local(): lax.all_to_all(weights, 'ep', split_axis=0, concat_axis=0, tiled=True)  19.8 us
    all_gather x1, waiting for transfers between devices, local(): arrived = lax.all_gather(token_acts[0], 'edp', axis=0, tiled=True)  18 us
    all_to_all x1, waiting for transfers between devices, local(): lax.all_to_all(second_old, 'ep', split_axis=0, concat_axis=0, tiled=True)  12.1 us
    all_to_all x1, waiting for transfers between devices, local(): lax.all_to_all(placed_steps, 'ep', split_axis=0, concat_axis=0, tiled=True)  12.1 us
    all_to_all x1, waiting for transfers between devices, local(): lax.all_to_all(placed_second, 'ep', split_axis=0, concat_axis=0, tiled=True)  11.1 us
    all_to_all x1, waiting for transfers between devices, local(): lax.all_to_all(first_old, 'ep', split_axis=0, concat_axis=0, tiled=True)  10.7 us
  transfers between devices with their start and end apart: 8, of which 7 were waited for; matrix products, arithmetic and copies ran while one was open for 14% of the time, Pallas kernels for 0%

commit v1 on v0

--- a/solution.py
+++ b/solution.py
@@ -52,7 +52,11 @@
         concat_axis=0,
         tiled=True,
     )
-    arrived = lax.all_gather(token_acts[0], "edp", axis=0, tiled=True)
+    own = token_acts[0]
+    size = lax.axis_size("edp")
+    blocks = jnp.stack([own for _ in range(size)])
+    blocks = lax.all_to_all(blocks, "edp", split_axis=0, concat_axis=0)
+    arrived = jnp.concatenate(blocks, axis=0)
     count_here = arrived.shape[0]
     grad_block = received
     grad_block = grad_block.reshape(count_here, row_count, slot_count, tok_slot)

time: 282 us -> 345 us (1.22)
  waiting for transfers between devices: 94.3 us -> 169 us
  between operations: 14.3 us -> 0.93 us
  blocking collectives: 66.9 us -> 60.4 us
  starting transfers between devices: 43.4 us -> 47.7 us
  local copies, waits for them, and re-layouts: 28.2 us -> 31.7 us
    all_to_all x0 -> x1, waiting for transfers between devices: none -> 93.7 us  [local(): blocks = lax.all_to_all(blocks, 'edp', split_axis=0, concat_axis=0)]
    all_gather x1 -> x0, waiting for transfers between devices: 18 us -> none  [local(): arrived = lax.all_gather(token_acts[0], 'edp', axis=0, tiled=True)]
    all_to_all x1, blocking collectives: 41 us -> 35.1 us  [local(): lax.all_to_all(masked.reshape(groups, row_count, slot_count * tok_slot),...]
    all_to_all x0 -> x1, starting transfers between devices: none -> 4.53 us  [local(): blocks = lax.all_to_all(blocks, 'edp', split_axis=0, concat_axis=0)]
    all_to_all x1, starting transfers between devices: 9.78 us -> 5.57 us  [local(): lax.all_to_all(second_old, 'ep', split_axis=0, concat_axis=0, tiled=True)]
    all_to_all x1, starting transfers between devices: 5.74 us -> 9.78 us  [local(): lax.all_to_all(first_old, 'ep', split_axis=0, concat_axis=0, tiled=True)]
    another operation x0 -> x1, local copies, waits for them, and re-layouts: none -> 3.45 us  [local(): blocks = jnp.stack([own for _ in range(size)])]
  transfers between devices with their start and end apart: 8 -> 8, of which waited for: 7 -> 7; matrix products, arithmetic and copies ran while one was open for 14% -> 11% of each run, Pallas kernels for 0% -> 0%
where the time goes in v1:
time: 345 us; the launch traced here: 343 us
  waiting for transfers between devices  169 us (49%)
  blocking collectives  60.4 us (18%)
  starting transfers between devices  47.7 us (14%)
  local copies, waits for them, and re-layouts  31.7 us (9%)
  other arithmetic  28.2 us (8%)
  matrix products  4.96 us (1%)
    all_to_all x1, waiting for transfers between devices, local(): blocks = lax.all_to_all(blocks, 'edp', split_axis=0, concat_axis=0)  93.7 us
    all_to_all x1, blocking collectives, local(): lax.all_to_all(masked.reshape(groups, row_count, slot_count * tok_slot),...  35.1 us
    all_to_all x1, blocking collectives, local(): lax.all_to_all(replica_grad.astype(jnp.bfloat16), 'ep', split_axis=0, con...  25.3 us
    all_to_all x1, waiting for transfers between devices, local(): lax.all_to_all(weights, 'ep', split_axis=0, concat_axis=0, tiled=True)  19.8 us
    all_to_all x1, waiting for transfers between devices, local(): lax.all_to_all(placed_steps, 'ep', split_axis=0, concat_axis=0, tiled=True)  12.1 us
    all_to_all x1, waiting for transfers between devices, local(): lax.all_to_all(first_old, 'ep', split_axis=0, concat_axis=0, tiled=True)  12.1 us
    all_to_all x1, waiting for transfers between devices, local(): lax.all_to_all(placed_first, 'ep', split_axis=0, concat_axis=0, tiled=True)  11.1 us
    all_to_all x1, waiting for transfers between devices, local(): lax.all_to_all(second_old, 'ep', split_axis=0, concat_axis=0, tiled=True)  10.7 us
  transfers between devices with their start and end apart: 8, of which 7 were waited for; matrix products, arithmetic and copies ran while one was open for 11% of the time, Pallas kernels for 0%

profile of v1, /device:TPU:2, one launch (start us, length us, event | category | flops | bytes accessed | tf_op | source)
XLA Modules:
  0.0 343.2 jit_solution(15834259271180663849)
XLA Ops:
  4.5 35.1 %all_to_all.82 = bf16[16,224,128]{2,1,0:T(8,128)(2,1)S(1)} all-to-all(bf16[16,224,128]{2,1,0:T(8,128)(2,1)S(1)} %broadcast_select_fusion), channel_id=1, replica_groups=mesh['edp'=16,'ep'=32] {'edp'}, dimensions={0} | all-to-all | bytes 1835008 | tf_op jit(solution)/shard_map/all_to_all | solution.py:48
  39.6 3.5 %stack.3 = bf16[16,1,2,64,1024]{4,3,2,1,0:T(8,128)(2,1)} broadcast(bf16[2,64,1024]{2,1,0:T(8,128)(2,1)} %bitcast.35), dimensions={2,3,4} | broadcast | bytes 4456448 | tf_op jit(solution)/shard_map/stack | solution.py:57
  43.1 4.5 %all-to-all-start.1 = ((bf16[16,1,2,64,1024]{4,3,2,1,0:T(8,128)(2,1)}), bf16[16,1,2,64,1024]{4,3,2,1,0:T(8,128)(2,1)}, u32[]{:S(2)}, u32[]{:S(2)}) async-start(bf16[16,1,2,64,1024]{4,3,2,1,0:T(8,128)(2,1)} %stack.3), calls=%async_computation.1 | async-start | bytes 8388608 | tf_op jit(solution)/shard_map/all_to_all | solution.py:58
  48.1 93.7 %all-to-all-done.1 = bf16[16,1,2,64,1024]{4,3,2,1,0:T(8,128)(2,1)} async-done(((bf16[16,1,2,64,1024]{4,3,2,1,0:T(8,128)(2,1)}), bf16[16,1,2,64,1024]{4,3,2,1,0:T(8,128)(2,1)}, u32[]{:S(2)}, u32[]{:S(2)}) %all-to-all-start.1) | async-done | bytes 4194336 | tf_op jit(solution)/shard_map/all_to_all | solution.py:58
  141.9 3.3 fusion.5
  146.3 3.3 reduce.3
  149.9 25.3 %all_to_all.83 = bf16[32,2,3584]{2,1,0:T(2,128)(2,1)S(1)} all-to-all(bf16[32,2,3584]{2,1,0:T(2,128)(2,1)S(1)} %reshape.150), channel_id=1, replica_groups=mesh['edp'=16,'ep'=32] {'ep'}, dimensions={0} | all-to-all | bytes 917504 | tf_op jit(solution)/shard_map/all_to_all | solution.py:73
  177.8 5.6 %all-to-all-start.3 = ((bf16[32,2,3584]{2,1,0:T(2,128)(2,1)}), bf16[32,2,3584]{2,1,0:T(2,128)(2,1)S(1)}, u32[]{:S(2)}, u32[]{:S(2)}) async-start(bf16[32,2,3584]{2,1,0:T(2,128)(2,1)} %reshape.152), calls=%async_computation.3 | async-start | bytes 917504 | tf_op jit(solution)/shard_map/all_to_all | solution.py:77
  183.4 2.1 convert_multiply_fusion.1
  187.1 2.1 convert_multiply_fusion
  189.1 2.5 mul.71
  191.6 2.2 broadcast_multiply_fusion
  193.9 2.6 mul.76
  200.2 3.1 fusion.32
  203.3 1.9 reduce.5
  206.3 9.8 %all-to-all-start.6 = ((bf16[32,2,3584]{2,1,0:T(2,128)(2,1)}), bf16[32,2,3584]{2,1,0:T(2,128)(2,1)S(1)}, u32[]{:S(2)}, u32[]{:S(2)}) async-start(bf16[32,2,3584]{2,1,0:T(2,128)(2,1)} %reshape.154), calls=%async_computation.6 | async-start | bytes 917504 | tf_op jit(solution)/shard_map/all_to_all | solution.py:85
  218.0 12.1 %all-to-all-done.6 = bf16[32,2,3584]{2,1,0:T(2,128)(2,1)S(1)} async-done(((bf16[32,2,3584]{2,1,0:T(2,128)(2,1)}), bf16[32,2,3584]{2,1,0:T(2,128)(2,1)S(1)}, u32[]{:S(2)}, u32[]{:S(2)}) %all-to-all-start.6) | async-done | bytes 458784 | tf_op jit(solution)/shard_map/all_to_all | solution.py:85
  230.1 5.6 %all-to-all-start.8 = ((bf16[32,2,3584]{2,1,0:T(2,128)(2,1)}), bf16[32,2,3584]{2,1,0:T(2,128)(2,1)S(1)}, u32[]{:S(2)}, u32[]{:S(2)}) async-start(bf16[32,2,3584]{2,1,0:T(2,128)(2,1)} %reshape.158), calls=%async_computation.8 | async-start | bytes 917504 | tf_op jit(solution)/shard_map/all_to_all | solution.py:86
  238.3 10.7 %all-to-all-done.8 = bf16[32,2,3584]{2,1,0:T(2,128)(2,1)S(1)} async-done(((bf16[32,2,3584]{2,1,0:T(2,128)(2,1)}), bf16[32,2,3584]{2,1,0:T(2,128)(2,1)S(1)}, u32[]{:S(2)}, u32[]{:S(2)}) %all-to-all-start.8) | async-done | bytes 458784 | tf_op jit(solution)/shard_map/all_to_all | solution.py:86
  249.1 5.6 %all-to-all-start.7 = ((bf16[32,2,3584]{2,1,0:T(2,128)(2,1)}), bf16[32,2,3584]{2,1,0:T(2,128)(2,1)S(1)}, u32[]{:S(2)}, u32[]{:S(2)}) async-start(bf16[32,2,3584]{2,1,0:T(2,128)(2,1)} %reshape.156), calls=%async_computation.7 | async-start | bytes 917504 | tf_op jit(solution)/shard_map/all_to_all | solution.py:98
  254.6 1.9 copy.32
  256.5 11.1 %all-to-all-done.7 = bf16[32,2,3584]{2,1,0:T(2,128)(2,1)S(1)} async-done(((bf16[32,2,3584]{2,1,0:T(2,128)(2,1)}), bf16[32,2,3584]{2,1,0:T(2,128)(2,1)S(1)}, u32[]{:S(2)}, u32[]{:S(2)}) %all-to-all-start.7) | async-done | bytes 458784 | tf_op jit(solution)/shard_map/all_to_all | solution.py:98
  267.6 5.6 %all-to-all-start.4 = ((f32[32,1,7168]{2,1,0:T(1,128)}), f32[32,1,7168]{2,1,0:T(1,128)S(1)}, u32[]{:S(2)}, u32[]{:S(2)}) async-start(f32[32,1,7168]{2,1,0:T(1,128)} %copy.32), calls=%async_computation.4 | async-start | bytes 1835008 | tf_op jit(solution)/shard_map/all_to_all | solution.py:83
  275.9 19.8 %all-to-all-done.4 = f32[32,1,7168]{2,1,0:T(1,128)S(1)} async-done(((f32[32,1,7168]{2,1,0:T(1,128)}), f32[32,1,7168]{2,1,0:T(1,128)S(1)}, u32[]{:S(2)}, u32[]{:S(2)}) %all-to-all-start.4) | async-done | bytes 917536 | tf_op jit(solution)/shard_map/all_to_all | solution.py:83
  295.6 5.6 %all-to-all-start.9 = ((bf16[32,2,3584]{2,1,0:T(2,128)(2,1)}), bf16[32,2,3584]{2,1,0:T(2,128)(2,1)S(1)}, u32[]{:S(2)}, u32[]{:S(2)}) async-start(bf16[32,2,3584]{2,1,0:T(2,128)(2,1)} %reshape.160), calls=%async_computation.9 | async-start | bytes 917504 | tf_op jit(solution)/shard_map/all_to_all | solution.py:99
  301.9 1.9 copy.33
  303.7 9.8 %all-to-all-done.9 = bf16[32,2,3584]{2,1,0:T(2,128)(2,1)S(1)} async-done(((bf16[32,2,3584]{2,1,0:T(2,128)(2,1)}), bf16[32,2,3584]{2,1,0:T(2,128)(2,1)S(1)}, u32[]{:S(2)}, u32[]{:S(2)}) %all-to-all-start.9) | async-done | bytes 458784 | tf_op jit(solution)/shard_map/all_to_all | solution.py:99
  313.5 5.6 %all-to-all-start.5 = ((f32[32,1,7168]{2,1,0:T(1,128)}), f32[32,1,7168]{2,1,0:T(1,128)S(1)}, u32[]{:S(2)}, u32[]{:S(2)}) async-start(f32[32,1,7168]{2,1,0:T(1,128)} %copy.33), calls=%async_computation.5 | async-start | bytes 1835008 | tf_op jit(solution)/shard_map/all_to_all | solution.py:96
  319.5 2.7 reduce.1
  323.8 2.7 reduce.2
  327.9 12.1 %all-to-all-done.5 = f32[32,1,7168]{2,1,0:T(1,128)S(1)} async-done(((f32[32,1,7168]{2,1,0:T(1,128)}), f32[32,1,7168]{2,1,0:T(1,128)S(1)}, u32[]{:S(2)}, u32[]{:S(2)}) %all-to-all-start.5) | async-done | bytes 917536 | tf_op jit(solution)/shard_map/all_to_all | solution.py:96
  340.0 2.2 reduce
  (40 shorter events, 27.0 us)
Async XLA Ops:
  43.1 98.8 %all-to-all-start.1 = ((bf16[16,1,2,64,1024]{4,3,2,1,0:T(8,128)(2,1)}), bf16[16,1,2,64,1024]{4,3,2,1,0:T(8,128)(2,1)}, u32[]{:S(2)}, u32[]{:S(2)}) async-start(bf16[16,1,2,64,1024]{4,3,2,1,0:T(8,128)(2,1)} %stack.3), calls=%async_computation.1 | async-start | bytes 8388608 | tf_op jit(solution)/shard_map/all_to_all | solution.py:58
  145.2 30.3 %copy-start = (s32[32]{0:T(128)S(1)}, s32[32]{0:T(128)}, u32[]{:S(2)}) copy-start(s32[32]{0:T(128)} %param.15) | copy-start | bytes 388
  145.3 30.3 %copy-start.2 = (s32[32]{0:T(128)S(1)}, s32[32]{0:T(128)}, u32[]{:S(2)}) copy-start(s32[32]{0:T(128)} %param.16) | copy-start | bytes 388
  177.8 21.2 %all-to-all-start.3 = ((bf16[32,2,3584]{2,1,0:T(2,128)(2,1)}), bf16[32,2,3584]{2,1,0:T(2,128)(2,1)S(1)}, u32[]{:S(2)}, u32[]{:S(2)}) async-start(bf16[32,2,3584]{2,1,0:T(2,128)(2,1)} %reshape.152), calls=%async_computation.3 | async-start | bytes 917504 | tf_op jit(solution)/shard_map/all_to_all | solution.py:77
  203.3 32.7 %copy-start.1 = (s32[32]{0:T(128)S(1)}, s32[32]{0:T(128)}, u32[]{:S(2)}) copy-start(s32[32]{0:T(128)} %param.17) | copy-start | bytes 388
  206.3 23.8 %all-to-all-start.6 = ((bf16[32,2,3584]{2,1,0:T(2,128)(2,1)}), bf16[32,2,3584]{2,1,0:T(2,128)(2,1)S(1)}, u32[]{:S(2)}, u32[]{:S(2)}) async-start(bf16[32,2,3584]{2,1,0:T(2,128)(2,1)} %reshape.154), calls=%async_computation.6 | async-start | bytes 917504 | tf_op jit(solution)/shard_map/all_to_all | solution.py:85
  230.1 19.0 %all-to-all-start.8 = ((bf16[32,2,3584]{2,1,0:T(2,128)(2,1)}), bf16[32,2,3584]{2,1,0:T(2,128)(2,1)S(1)}, u32[]{:S(2)}, u32[]{:S(2)}) async-start(bf16[32,2,3584]{2,1,0:T(2,128)(2,1)} %reshape.158), calls=%async_computation.8 | async-start | bytes 917504 | tf_op jit(solution)/shard_map/all_to_all | solution.py:86
  249.1 18.6 %all-to-all-start.7 = ((bf16[32,2,3584]{2,1,0:T(2,128)(2,1)}), bf16[32,2,3584]{2,1,0:T(2,128)(2,1)S(1)}, u32[]{:S(2)}, u32[]{:S(2)}) async-start(bf16[32,2,3584]{2,1,0:T(2,128)(2,1)} %reshape.156), calls=%async_computation.7 | async-start | bytes 917504 | tf_op jit(solution)/shard_map/all_to_all | solution.py:98
  267.6 28.0 %all-to-all-start.4 = ((f32[32,1,7168]{2,1,0:T(1,128)}), f32[32,1,7168]{2,1,0:T(1,128)S(1)}, u32[]{:S(2)}, u32[]{:S(2)}) async-start(f32[32,1,7168]{2,1,0:T(1,128)} %copy.32), calls=%async_computation.4 | async-start | bytes 1835008 | tf_op jit(solution)/shard_map/all_to_all | solution.py:83
  295.6 17.8 %all-to-all-start.9 = ((bf16[32,2,3584]{2,1,0:T(2,128)(2,1)}), bf16[32,2,3584]{2,1,0:T(2,128)(2,1)S(1)}, u32[]{:S(2)}, u32[]{:S(2)}) async-start(bf16[32,2,3584]{2,1,0:T(2,128)(2,1)} %reshape.160), calls=%async_computation.9 | async-start | bytes 917504 | tf_op jit(solution)/shard_map/all_to_all | solution.py:99
  313.5 26.5 %all-to-all-start.5 = ((f32[32,1,7168]{2,1,0:T(1,128)}), f32[32,1,7168]{2,1,0:T(1,128)S(1)}, u32[]{:S(2)}, u32[]{:S(2)}) async-start(f32[32,1,7168]{2,1,0:T(1,128)} %copy.33), calls=%async_computation.5 | async-start | bytes 1835008 | tf_op jit(solution)/shard_map/all_to_all | solution.py:96
